TPU v7x, 32 devices: a whole 2x2x4 slice. The times are simulated.
32 devices in a mesh: grp: 2 (over x), ctx: 16 (over z, y, core).
Axes of the slice: x: 2, y: 2, z: 4, core: 2. Of those that a mesh axis runs over, the one named last changes fastest.
Arguments:
- queries: bfloat16 [4, 12, 64, 128], P(None, 'grp'), parts along dimension 1, may hold values from -150 to 150
- key_cache: bfloat16 [12, 8, 2048, 128], P('grp', None, 'ctx'), parts along dimension 0, may hold values from -6 to 6
- value_cache: bfloat16 [12, 8, 2048, 128], P('grp', None, 'ctx'), parts along dimension 0, may hold values from -6 to 6
- row_lengths: int32 [12], P('grp'), parts along dimension 0, may hold values from 128 to 2048, as said below
- kept_tiles: int32 [4, 12, 16], P(None, 'grp'), parts along dimension 1, may hold values from 0 to 1, as said below
- tile_dest: int32 [12, 8, 16], P('grp'), parts along dimension 0, may hold values from 0 to 15, as said below
Outputs:
- attn_out: bfloat16 [4, 12, 64, 128], P(None, 'grp'), parts along dimension 1
- tile_mass: float32 [12, 8, 16], P('grp', None, 'ctx'), parts along dimension 0
- moved_keys: bfloat16 [12, 8, 2048, 128], P('grp', None, 'ctx'), parts along dimension 0
- moved_values: bfloat16 [12, 8, 2048, 128], P('grp', None, 'ctx'), parts along dimension 0
There are 2 independent parts, one for each index of `grp`. A program takes and returns all parts, laid end to end along the dimension named above; each array names one. Nothing has to cross between parts.
Inputs may be any that keep to these rules, and one draw needn't show every extreme that they name: `row_lengths`: at least 128 positions of every row are filled; some row is filled to all 2048 positions. `kept_tiles`: A tile dropped at one step stays dropped at all later steps; tile 0 of every row is kept at every step. For each row and head, tile_dest is a permutation of the 16 tiles. The 1 tiles that one index of ctx holds for a row and head all go, in some order, to the index a per-row-and-head offset further along ctx, wrapping around; that offset is the same for every index. No offset is used by more than 3 row-head pairs, and some offset is used by exactly 3. The offsets 16 // 2 and 1 are used by some row-head pair in every draw.
All inputs are finite; a program needn't handle non-finite values.
Results may differ from a plain program's by a relative error of at most 0.0027.
Values may be sent and summed in bfloat16 or wider, within the bound.
A program may use at most 64 MiB of HBM per device.

v0:
```python
import functools

import jax
import jax.numpy as jnp
from jax import lax
from jax.experimental import pallas as pl
from jax.experimental.pallas import tpu as pltpu
from jax.sharding import PartitionSpec as P

QH = 64
KVH = 8
HD = 128
TILE = 128
STEPS = 4
LANES = 128
STAT_ROWS = 8
MOVE_CUTS = (5, 5, 9, 15)

absent_score = -1e30


def fold_stats(peaks, totals):
    top = functools.reduce(jnp.maximum, peaks)
    factors = [jnp.exp(peak - top) for peak in peaks]
    total = sum(factor * part for factor, part in zip(factors, totals))
    return top, total, factors


def columns_of(rows):
    height = len(rows)
    filler = jnp.zeros((LANES - height, LANES), jnp.float32)
    return jnp.transpose(jnp.concatenate(list(rows) + [filler], axis=0))


def stat_block(top, total):
    return jnp.concatenate([top, total, jnp.zeros((STAT_ROWS - 2, LANES), jnp.float32)], axis=0)


def main_kernel(
    device_count, plane, group_count,
    order_ref, lengths_ref, kept_ref, queries_hbm, keys_hbm, values_hbm,
    arrived_ref, attn_ref, mass_ref,
    queries_ref, keys_ref, values_ref, load_sem, staged, parts, columns, stats, parts_in, stats_in, merged, merged_stats,
    merged_in, merged_stats_in, final, final_stats,
    own_sem, move_send, move_recv, a_send, a_recv, b_send, b_recv, c_send, c_recv, d_send, d_recv,
):
    me = lax.axis_index("ctx")
    outer = device_count // plane
    row_count, head_count = keys_ref.shape[:2]
    pair_count = row_count * head_count
    steps = queries_ref.shape[0]
    group_size = queries_ref.shape[2] // head_count
    pair_rows = steps * group_size
    owner_rows = group_count * pair_rows
    my_outer = me // plane
    my_column = me % plane

    barrier = pltpu.get_barrier_semaphore()
    for step in range(1, device_count):
        pl.semaphore_signal(barrier, inc=1, device_id={"ctx": (me + step) % device_count})

    loads = [
        pltpu.make_async_copy(src, dst, load_sem.at[which])
        for which, (src, dst) in enumerate(
            ((keys_hbm, keys_ref), (values_hbm, values_ref), (queries_hbm, queries_ref))
        )
    ]
    for load in loads:
        load.start()
    for load in loads:
        load.wait()

    @pl.loop(0, device_count * group_count)
    def _(slot):
        pair = order_ref[slot]
        row, head = pair // head_count, pair % head_count
        staged[slot, 0] = keys_ref[row, head]
        staged[slot, 1] = values_ref[row, head]

    pl.semaphore_wait(barrier, device_count - 1)

    own = pltpu.make_async_copy(
        staged.at[pl.ds(0, group_count)], arrived_ref.at[pl.ds(0, group_count)], own_sem
    )
    own.start()

    def move(level_step, half_flip, side_flip):
        level = (my_outer + jnp.where(my_outer < outer // 2, level_step, outer - level_step)) % outer
        half, side = my_column // sides, my_column % sides
        column = (half + half_flip) % halves * sides + (side + side_flip) % sides
        target = level * plane + column
        offset = (target - me + device_count) % device_count
        window = pl.ds(offset * group_count, group_count)
        return pltpu.make_async_remote_copy(
            src_ref=staged.at[window],
            dst_ref=arrived_ref.at[window],
            send_sem=move_send.at[offset],
            recv_sem=move_recv.at[offset],
            device_id={"ctx": target},
        )

    halves = 2 if plane % 2 == 0 else 1
    sides = plane // halves
    turns = [
        (level_step, half_flip, side_flip)
        for half_flip in range(halves)
        for level_step in list(range(half_flip, outer)) + [0] * half_flip
        for side_flip in range(sides)
    ][1:]

    def start_moves(first, last):
        for turn in turns[first:last]:
            move(*turn).start()

    cuts = [0] + [len(turns) * part // 15 for part in MOVE_CUTS] + [len(turns)]
    start_moves(cuts[0], cuts[1])

    lane = lax.broadcasted_iota(jnp.int32, (pair_rows, TILE), 1)
    step_of = lax.broadcasted_iota(jnp.int32, (pair_rows, TILE), 0) // group_size
    if device_count * group_count > pair_count:
        parts[...] = jnp.zeros_like(parts)
    columns[...] = jnp.zeros_like(columns)

    @pl.loop(0, row_count)
    def _(row):
        filled = lengths_ref[row] - me * TILE
        limit = jnp.zeros((pair_rows, TILE), jnp.int32)
        for step in range(steps):
            here = jnp.where(kept_ref[row, step, me] > 0, filled, 0)
            limit = jnp.where(step_of == step, here, limit)
        live = lane < limit
        query_rows = [queries_ref[step, row].astype(jnp.float32) for step in range(steps)]
        scores = []
        for head in range(head_count):
            span = slice(head * group_size, (head + 1) * group_size)
            query = jnp.concatenate([q[span] for q in query_rows], axis=0).astype(jnp.bfloat16)
            scores.append(lax.dot_general(
                query, keys_ref[row, head], (((1,), (1,)), ((), ())),
                preferred_element_type=jnp.float32,
            ))
        scores = jnp.stack(scores) * HD ** (-0.5)
        peak = jnp.max(jnp.where(live[None], scores, absent_score), axis=2, keepdims=True)
        weights = jnp.where(live[None], jnp.exp(scores - peak), 0.0)
        total = jnp.sum(weights, axis=2, keepdims=True)
        both = jnp.where(lane[None] == 0, peak, total)
        rounded = weights.astype(jnp.bfloat16)
        for head in range(head_count):
            pair = row * head_count + head
            owner, slot = pair // group_count, pair % group_count
            place = pl.ds(pl.multiple_of(slot * pair_rows, pair_rows), pair_rows)
            parts[owner % plane, owner // plane, place] = jnp.dot(
                rounded[head], values_ref[row, head], preferred_element_type=jnp.float32
            )
            columns[owner, place] = both[head]

    @pl.loop(0, device_count)
    def _(owner):
        turned = jnp.transpose(columns[owner])
        stats[owner % plane, owner // plane] = turned[:STAT_ROWS]

    sends_a = []
    for step in range(1, plane):
        peer = (my_column + step) % plane
        target = my_outer * plane + peer
        for which, (src, dst) in enumerate(((parts, parts_in), (stats, stats_in))):
            sends_a.append(pltpu.make_async_remote_copy(
                src_ref=src.at[peer], dst_ref=dst.at[step - 1],
                send_sem=a_send.at[which, step - 1], recv_sem=a_recv.at[which, step - 1],
                device_id={"ctx": target},
            ))
    for copy in sends_a:
        copy.start()
    start_moves(cuts[1], cuts[2])
    for copy in sends_a:
        copy.wait_recv()

    @pl.loop(0, outer)
    def _(level):
        blocks = [stats[my_column, level]] + [stats_in[k, level] for k in range(plane - 1)]
        top, total, factors = fold_stats([b[0:1] for b in blocks], [b[1:2] for b in blocks])
        scale = columns_of(factors)[:owner_rows]
        summed = scale[:, 0:1] * parts[my_column, level]
        for k in range(plane - 1):
            summed += scale[:, k + 1 : k + 2] * parts_in[k, level]
        merged[level] = summed
        merged_stats[level] = stat_block(top, total)

    sends_b = []
    for step in range(1, outer):
        level = (my_outer + step) % outer
        for which, (src, dst) in enumerate(((merged, merged_in), (merged_stats, merged_stats_in))):
            sends_b.append(pltpu.make_async_remote_copy(
                src_ref=src.at[level], dst_ref=dst.at[step - 1],
                send_sem=b_send.at[which, step - 1], recv_sem=b_recv.at[which, step - 1],
                device_id={"ctx": level * plane + my_column},
            ))
    for copy in sends_b:
        copy.start()
    start_moves(cuts[2], cuts[3])
    for copy in sends_b:
        copy.wait_recv()

    blocks = [merged_stats[my_outer]] + [merged_stats_in[k] for k in range(outer - 1)]
    top, total, factors = fold_stats([b[0:1] for b in blocks], [b[1:2] for b in blocks])
    scale = columns_of(factors + [total])[:owner_rows]
    summed = scale[:, 0:1] * merged[my_outer]
    for k in range(outer - 1):
        summed += scale[:, k + 1 : k + 2] * merged_in[k]
    final[my_column, my_outer] = (summed / scale[:, outer : outer + 1]).astype(jnp.bfloat16)
    final_stats[my_column, my_outer] = stat_block(top, total)

    sends_c = []
    for step in range(1, outer):
        level = (my_outer + step) % outer
        for which, ref in enumerate((final, final_stats)):
            sends_c.append(pltpu.make_async_remote_copy(
                src_ref=ref.at[my_column, my_outer], dst_ref=ref.at[my_column, my_outer],
                send_sem=c_send.at[which, step - 1], recv_sem=c_recv.at[which, step - 1],
                device_id={"ctx": level * plane + my_column},
            ))
    for copy in sends_c:
        copy.start()
    start_moves(cuts[3], cuts[4])
    for copy in sends_c:
        copy.wait_recv()
    sends_d = []
    for step in range(1, plane):
        target = my_outer * plane + (my_column + step) % plane
        for which, ref in enumerate((final, final_stats)):
            sends_d.append(pltpu.make_async_remote_copy(
                src_ref=ref.at[my_column], dst_ref=ref.at[my_column],
                send_sem=d_send.at[which, step - 1], recv_sem=d_recv.at[which, step - 1],
                device_id={"ctx": target},
            ))
    for copy in sends_d:
        copy.start()
    start_moves(cuts[4], cuts[5])
    for copy in sends_d:
        copy.wait_recv()

    for row in range(row_count):
        pieces = []
        for head in range(head_count):
            owner, slot = divmod(row * head_count + head, group_count)
            span = slice(slot * pair_rows, (slot + 1) * pair_rows)
            pieces.append(final[owner % plane, owner // plane, span].astype(jnp.float32))
        for step in range(steps):
            span = slice(step * group_size, (step + 1) * group_size)
            attn_ref[step, row] = jnp.concatenate([p[span] for p in pieces], axis=0).astype(jnp.bfloat16)

    group_of = lax.broadcasted_iota(jnp.int32, (1, LANES), 1) // pair_rows
    masses = []
    for pair in range(pair_count):
        owner, slot = divmod(pair, group_count)
        own_stats = stats[owner % plane, owner // plane]
        all_stats = final_stats[owner % plane, owner // plane]
        factor = jnp.exp(own_stats[0:1] - all_stats[0:1])
        mass = own_stats[1:2] * factor / all_stats[1:2]
        masses.append(jnp.where(group_of == slot, mass, 0.0))
    mass_row = jnp.sum(columns_of(masses), axis=0, keepdims=True)
    for row in range(row_count):
        mass_ref[row] = mass_row[:, row * head_count : (row + 1) * head_count]

    own.wait()
    for copy in sends_a + sends_b + sends_c + sends_d:
        copy.wait_send()
    for turn in turns:
        move(*turn).wait_send()
    for turn in turns:
        move(*turn).wait_recv()


def place_kernel(
    slot_ref, arrived_hbm, attn_ref, mass_ref, keys_out, values_out, attn_out, mass_out,
    arrived_ref, keys_ref, values_ref, attn_held, in_sem, out_sem,
):
    row_count, head_count = keys_out.shape[:2]
    loads = [
        pltpu.make_async_copy(arrived_hbm.at[:, which], arrived_ref.at[which], in_sem.at[which])
        for which in range(2)
    ]
    for load in loads:
        load.start()
    small = pltpu.make_async_copy(attn_ref, attn_held, in_sem.at[2])
    small.start()
    mass_out[...] = mass_ref[...]
    small.wait()
    out = [pltpu.make_async_copy(attn_held, attn_out, out_sem.at[2, 0])]
    out[0].start()
    for which, (held, placed) in enumerate(((keys_ref, keys_out), (values_ref, values_out))):
        loads[which].wait()
        for row in range(row_count):
            for head in range(head_count):
                held[row, head] = arrived_ref[which, slot_ref[row * head_count + head]]
            out.append(pltpu.make_async_copy(held.at[row], placed.at[row], out_sem.at[which, row]))
            out[-1].start()
    for copy in out:
        copy.wait()


def local(queries, key_cache, value_cache, row_lengths, kept_tiles, tile_dest):
    device_count = lax.axis_size("ctx")
    plane = 4 if device_count % 4 == 0 and device_count > 4 else 1
    outer = device_count // plane
    row_count, head_count, token_span, width = key_cache.shape
    pair_count = row_count * head_count
    group_count = -(-pair_count // device_count)
    pair_rows = STEPS * (QH // head_count)
    owner_rows = group_count * pair_rows
    slots = device_count * group_count
    assert owner_rows <= LANES and token_span == TILE

    offsets = (tile_dest[:, :, 0] % device_count).reshape(pair_count)
    index = jnp.arange(pair_count, dtype=jnp.int32)
    earlier = (index[:, None] > index[None, :]) & (offsets[:, None] == offsets[None, :])
    slot_of = offsets * group_count + jnp.sum(earlier.astype(jnp.int32), axis=1)
    hit = slot_of[:, None] == jnp.arange(slots, dtype=jnp.int32)[None, :]
    order = jnp.sum(jnp.where(hit, index[:, None], 0), axis=0)

    smem = pl.BlockSpec(memory_space=pltpu.SMEM)
    vmem = pl.BlockSpec(memory_space=pltpu.VMEM)
    hbm = pl.BlockSpec(memory_space=pltpu.HBM)
    sems = pltpu.SemaphoreType.DMA
    arrived, attn_out, mass = pl.pallas_call(
        functools.partial(main_kernel, device_count, plane, group_count),
        out_shape=(
            jax.ShapeDtypeStruct((slots, 2, TILE, width), jnp.bfloat16),
            jax.ShapeDtypeStruct(queries.shape, jnp.bfloat16),
            jax.ShapeDtypeStruct((row_count, 1, head_count), jnp.float32),
        ),
        in_specs=[smem, smem, smem, hbm, hbm, hbm],
        out_specs=(hbm, vmem, vmem),
        scratch_shapes=[
            pltpu.VMEM(queries.shape, jnp.bfloat16),
            pltpu.VMEM(key_cache.shape, jnp.bfloat16),
            pltpu.VMEM(value_cache.shape, jnp.bfloat16),
            sems((3,)),
            pltpu.VMEM((slots, 2, TILE, width), jnp.bfloat16),
            pltpu.VMEM((plane, outer, owner_rows, width), jnp.float32),
            pltpu.VMEM((device_count, LANES, LANES), jnp.float32),
            pltpu.VMEM((plane, outer, STAT_ROWS, LANES), jnp.float32),
            pltpu.VMEM((plane - 1, outer, owner_rows, width), jnp.float32),
            pltpu.VMEM((plane - 1, outer, STAT_ROWS, LANES), jnp.float32),
            pltpu.VMEM((outer, owner_rows, width), jnp.float32),
            pltpu.VMEM((outer, STAT_ROWS, LANES), jnp.float32),
            pltpu.VMEM((outer - 1, owner_rows, width), jnp.float32),
            pltpu.VMEM((outer - 1, STAT_ROWS, LANES), jnp.float32),
            pltpu.VMEM((plane, outer, owner_rows, width), jnp.bfloat16),
            pltpu.VMEM((plane, outer, STAT_ROWS, LANES), jnp.float32),
            sems,
            sems((device_count,)),
            sems((device_count,)),
            sems((2, plane - 1)),
            sems((2, plane - 1)),
            sems((2, outer - 1)),
            sems((2, outer - 1)),
            sems((2, outer - 1)),
            sems((2, outer - 1)),
            sems((2, plane - 1)),
            sems((2, plane - 1)),
        ],
        compiler_params=pltpu.CompilerParams(
            collective_id=0, has_side_effects=True, vmem_limit_bytes=63 * 1024 * 1024
        ),
        name="attend_and_move",
    )(order, row_lengths, jnp.swapaxes(kept_tiles, 0, 1), queries, key_cache, value_cache)

    moved_keys, moved_values, attn_out, tile_mass = pl.pallas_call(
        place_kernel,
        out_shape=(
            jax.ShapeDtypeStruct(key_cache.shape, jnp.bfloat16),
            jax.ShapeDtypeStruct(value_cache.shape, jnp.bfloat16),
            jax.ShapeDtypeStruct(attn_out.shape, attn_out.dtype),
            jax.ShapeDtypeStruct(mass.shape, mass.dtype),
        ),
        in_specs=[smem, hbm, hbm, vmem],
        out_specs=(hbm, hbm, hbm, vmem),
        scratch_shapes=[
            pltpu.VMEM((2, slots, TILE, width), jnp.bfloat16),
            pltpu.VMEM(key_cache.shape, jnp.bfloat16),
            pltpu.VMEM(value_cache.shape, jnp.bfloat16),
            pltpu.VMEM(attn_out.shape, attn_out.dtype),
            sems((3,)),
            sems((3, row_count)),
        ],
        compiler_params=pltpu.CompilerParams(vmem_limit_bytes=63 * 1024 * 1024),
        name="place",
    )(slot_of, arrived, attn_out, mass)
    return attn_out, jnp.swapaxes(tile_mass, 1, 2), moved_keys, moved_values


def solution(mesh):
    in_specs = (
        P(None, "grp", None, None),
        P("grp", None, "ctx", None),
        P("grp", None, "ctx", None),
        P("grp"),
        P(None, "grp", None),
        P("grp", None, None),
    )
    out_specs = (
        P(None, "grp", None, None),
        P("grp", None, "ctx"),
        P("grp", None, "ctx", None),
        P("grp", None, "ctx", None),
    )
    return jax.shard_map(local, mesh=mesh, in_specs=in_specs, out_specs=out_specs, check_vma=False)
```

profile of v0, /device:TPU:1, one launch (start us, length us, event | category | flops | bytes accessed | tf_op | source)
XLA Modules:
  0.0 97.2 jit_solution(2125388934264020899)
XLA Ops:
  0.6 0.9 slice_reduce_fusion
  1.5 0.1 squeeze.3
  1.6 0.2 convert_reduce_fusion
  1.8 0.0 copy-start
  1.8 0.6 select_reduce_fusion.order_ref
  2.5 89.6 %attend_and_move.1 = (bf16[48,2,128,128]{3,2,1,0:T(8,128)(2,1)}, bf16[4,6,64,128]{3,2,1,0:T(8,128)(2,1)}, f32[6,1,8]{2,1,0:T(1,128)}) custom-call(s32[48]{0:T(128)} %select_reduce_fusion.order_ref, s32[6]{0:T(128)} %lengths_ref.1, s32[6,4,16]{2,1,0:T(4,128)} %bitcast.2, bf16[4,6,64,128]{3,2,1,0:T(8,128)(2,1)} %queries_hbm.1, ...), custom_call_target="tpu_custom_call" | custom-call | tf_op jit(solution)/shard_map/attend_and_move/pallas_call | solution.py:324
  92.0 0.0 copy-done
  92.0 5.2 %place.1 = (bf16[6,8,128,128]{3,2,1,0:T(8,128)(2,1)}, bf16[6,8,128,128]{3,2,1,0:T(8,128)(2,1)}, bf16[4,6,64,128]{3,2,1,0:T(8,128)(2,1)}, f32[6,1,8]{2,1,0:T(1,128)}) custom-call(s32[48]{0:T(128)} %copy-done, bf16[48,2,128,128]{3,2,1,0:T(8,128)(2,1)} %get-tuple-element.11.arrived_hbm, bf16[4,6,64,128]{3,2,1,0:T(8,128)(2,1)} %get-tuple-element.12.attn_ref, ...), custom_call_target="tpu_custom_call" | custom-call | tf_op jit(solution)/shard_map/place/pallas_call | solution.py:368
  (2 shorter events, 0.0 us)
Async XLA Ops:
  1.8 90.2 %copy-start = (s32[48]{0:T(128)}, s32[48]{0:T(128)S(1)}, u32[]{:S(2)}) copy-start(s32[48]{0:T(128)S(1)} %multiply_add_fusion.slot_ref) | copy-start | bytes 580
where the time goes:
time: 97.5 us; the launch traced here: 97.2 us
  Pallas kernels  94.7 us (97%)
  local copies, waits for them, and re-layouts  0.99 us (1%)
    pallas_call x1, Pallas kernels, local(): pl.pallas_call(functools.partial(main_kernel, device_count, plane, group_...  89.6 us
    pallas_call x1, Pallas kernels, local(): pl.pallas_call(place_kernel, out_shape=(jax.ShapeDtypeStruct(key_cache.sh...  5.18 us

commit v1 on v0

--- a/solution.py
+++ b/solution.py
@@ -14,7 +14,6 @@
 STEPS = 4
 LANES = 128
 STAT_ROWS = 8
-MOVE_CUTS = (5, 5, 9, 15)
 
 absent_score = -1e30
 
@@ -84,8 +83,16 @@
     )
     own.start()
 
-    def move(level_step, half_flip, side_flip):
-        level = (my_outer + jnp.where(my_outer < outer // 2, level_step, outer - level_step)) % outer
+    lower = my_outer < outer // 2
+    near_count = outer // 2 if outer % 2 == 0 else outer
+    mirrored = jnp.where(lower, my_outer, outer - 1 - my_outer)
+
+    def move(level_kind, level_index, half_flip, side_flip):
+        if level_kind == "far":
+            level = outer - 1 - level_index
+        else:
+            level = (mirrored + level_index) % near_count
+        level = jnp.where(lower, level, outer - 1 - level)
         half, side = my_column // sides, my_column % sides
         column = (half + half_flip) % halves * sides + (side + side_flip) % sides
         target = level * plane + column
@@ -101,19 +108,29 @@
 
     halves = 2 if plane % 2 == 0 else 1
     sides = plane // halves
-    turns = [
-        (level_step, half_flip, side_flip)
-        for half_flip in range(halves)
-        for level_step in list(range(half_flip, outer)) + [0] * half_flip
-        for side_flip in range(sides)
-    ][1:]
-
-    def start_moves(first, last):
-        for turn in turns[first:last]:
+    far = [("far", k) for k in range(outer - near_count)]
+    near = [("near", k) for k in range(1, near_count)]
+    own_level = [("near", 0)]
+    first_far, second_far = far[: len(far) // 2], far[len(far) // 2 :]
+
+    def to_columns(levels, half_flip):
+        if half_flip >= halves:
+            return []
+        return [(*level, half_flip, side) for side in range(sides) for level in levels]
+
+    batches = [
+        to_columns(first_far, 0) + to_columns(near, 0) + to_columns(own_level, 0)[1:],
+        to_columns(second_far, 0) + to_columns(near, 1)[: len(near)],
+        to_columns(first_far, 1) + to_columns(second_far, 1) + to_columns(near, 1)[len(near) :] + to_columns(own_level, 1),
+    ]
+    turns = [turn for batch in batches for turn in batch]
+    assert len(turns) == device_count - 1
+
+    def start_moves(batch):
+        for turn in batches[batch]:
             move(*turn).start()
 
-    cuts = [0] + [len(turns) * part // 15 for part in MOVE_CUTS] + [len(turns)]
-    start_moves(cuts[0], cuts[1])
+    start_moves(0)
 
     lane = lax.broadcasted_iota(jnp.int32, (pair_rows, TILE), 1)
     step_of = lax.broadcasted_iota(jnp.int32, (pair_rows, TILE), 0) // group_size
@@ -170,7 +187,6 @@
             ))
     for copy in sends_a:
         copy.start()
-    start_moves(cuts[1], cuts[2])
     for copy in sends_a:
         copy.wait_recv()
 
@@ -196,7 +212,7 @@
             ))
     for copy in sends_b:
         copy.start()
-    start_moves(cuts[2], cuts[3])
+    start_moves(1)
     for copy in sends_b:
         copy.wait_recv()
 
@@ -220,7 +236,7 @@
             ))
     for copy in sends_c:
         copy.start()
-    start_moves(cuts[3], cuts[4])
+    start_moves(2)
     for copy in sends_c:
         copy.wait_recv()
     sends_d = []
@@ -234,7 +250,6 @@
             ))
     for copy in sends_d:
         copy.start()
-    start_moves(cuts[4], cuts[5])
     for copy in sends_d:
         copy.wait_recv()
 

time: 97.5 us -> 91 us (0.933)
  the two profiles are of different devices: /device:TPU:1 before, /device:TPU:9 now
where the time goes in v1:
time: 91 us; the launch traced here: 90.7 us
  Pallas kernels  88.3 us (97%)
  local copies, waits for them, and re-layouts  0.99 us (1%)
    pallas_call x1, Pallas kernels, local(): pl.pallas_call(functools.partial(main_kernel, device_count, plane, group_...  83.1 us
    pallas_call x1, Pallas kernels, local(): pl.pallas_call(place_kernel, out_shape=(jax.ShapeDtypeStruct(key_cache.sh...  5.18 us

profile of v1, /device:TPU:9, one launch (start us, length us, event | category | flops | bytes accessed | tf_op | source)
XLA Modules:
  0.0 90.7 jit_solution(8406129146832854962)
XLA Ops:
  0.6 0.9 %slice_reduce_fusion = s32[6,8]{1,0:T(8,128)S(1)} fusion(s32[6,8,16]{2,1,0:T(8,128)} %param.11), kind=kLoop, calls=%fused_computation.4 | loop fusion | bytes 384 | tf_op jit(solution)/shard_map/slice | solution.py:328
  1.5 0.1 squeeze.3
  1.6 0.2 convert_reduce_fusion
  1.8 0.0 copy-start
  1.8 0.6 select_reduce_fusion.order_ref
  2.5 83.1 %attend_and_move.1 = (bf16[48,2,128,128]{3,2,1,0:T(8,128)(2,1)}, bf16[4,6,64,128]{3,2,1,0:T(8,128)(2,1)}, f32[6,1,8]{2,1,0:T(1,128)}) custom-call(s32[48]{0:T(128)} %select_reduce_fusion.order_ref, s32[6]{0:T(128)} %lengths_ref.1, s32[6,4,16]{2,1,0:T(4,128)} %bitcast.2, bf16[4,6,64,128]{3,2,1,0:T(8,128)(2,1)} %queries_hbm.1, ...), custom_call_target="tpu_custom_call" | custom-call | tf_op jit(solution)/shard_map/attend_and_move/pallas_call | solution.py:339
  85.5 0.0 copy-done
  85.6 5.2 %place.1 = (bf16[6,8,128,128]{3,2,1,0:T(8,128)(2,1)}, bf16[6,8,128,128]{3,2,1,0:T(8,128)(2,1)}, bf16[4,6,64,128]{3,2,1,0:T(8,128)(2,1)}, f32[6,1,8]{2,1,0:T(1,128)}) custom-call(s32[48]{0:T(128)} %copy-done, bf16[48,2,128,128]{3,2,1,0:T(8,128)(2,1)} %get-tuple-element.11.arrived_hbm, bf16[4,6,64,128]{3,2,1,0:T(8,128)(2,1)} %get-tuple-element.12.attn_ref, ...), custom_call_target="tpu_custom_call" | custom-call | tf_op jit(solution)/shard_map/place/pallas_call | solution.py:383
  (2 shorter events, 0.0 us)
Async XLA Ops:
  1.8 83.7 %copy-start = (s32[48]{0:T(128)}, s32[48]{0:T(128)S(1)}, u32[]{:S(2)}) copy-start(s32[48]{0:T(128)S(1)} %multiply_add_fusion.slot_ref) | copy-start | bytes 580

commit v2 on v1

--- a/solution.py
+++ b/solution.py
@@ -35,11 +35,26 @@
     return jnp.concatenate([top, total, jnp.zeros((STAT_ROWS - 2, LANES), jnp.float32)], axis=0)
 
 
+def slots_of(dest, group_count):
+    row_count, head_count, tiles = dest.shape
+    pair_count = row_count * head_count
+    offset = jnp.broadcast_to(dest.reshape(pair_count, tiles)[:, 0:1], (pair_count, LANES))
+    filler = jnp.full((LANES - pair_count, LANES), -1, jnp.int32)
+    across = jnp.transpose(jnp.concatenate([offset, filler], axis=0))[:pair_count]
+    pair = lax.broadcasted_iota(jnp.int32, (pair_count, LANES), 0)
+    lane = lax.broadcasted_iota(jnp.int32, (pair_count, LANES), 1)
+    earlier = jnp.where((offset == across) & (lane < pair), 1, 0)
+    slot = offset[:, 0:1] * group_count + jnp.sum(earlier, axis=1, keepdims=True)
+    order = jnp.sum(jnp.where(slot == lane, pair, 0), axis=0, keepdims=True)
+    spread = jnp.concatenate([jnp.broadcast_to(slot, (pair_count, LANES)), filler], axis=0)
+    return order, jnp.transpose(spread)[0:1]
+
+
 def main_kernel(
     device_count, plane, group_count,
-    order_ref, lengths_ref, kept_ref, queries_hbm, keys_hbm, values_hbm,
-    arrived_ref, attn_ref, mass_ref,
-    queries_ref, keys_ref, values_ref, load_sem, staged, parts, columns, stats, parts_in, stats_in, merged, merged_stats,
+    lengths_hbm, kept_hbm, dest_hbm, queries_hbm, keys_hbm, values_hbm,
+    arrived_ref, attn_ref, mass_ref, slot_ref,
+    lengths_ref, kept_ref, dest_ref, order_row, order_ref, order_sem, queries_ref, keys_ref, values_ref, load_sem, staged, parts, columns, stats, parts_in, stats_in, merged, merged_stats,
     merged_in, merged_stats_in, final, final_stats,
     own_sem, move_send, move_recv, a_send, a_recv, b_send, b_recv, c_send, c_recv, d_send, d_recv,
 ):
@@ -58,20 +73,31 @@
     for step in range(1, device_count):
         pl.semaphore_signal(barrier, inc=1, device_id={"ctx": (me + step) % device_count})
 
+    dest_load = pltpu.make_async_copy(dest_hbm, dest_ref, order_sem.at[0])
+    dest_load.start()
     loads = [
         pltpu.make_async_copy(src, dst, load_sem.at[which])
         for which, (src, dst) in enumerate(
-            ((keys_hbm, keys_ref), (values_hbm, values_ref), (queries_hbm, queries_ref))
+            (
+                (keys_hbm, keys_ref), (values_hbm, values_ref), (queries_hbm, queries_ref),
+                (lengths_hbm, lengths_ref), (kept_hbm, kept_ref),
+            )
         )
     ]
     for load in loads:
         load.start()
+
+    dest_load.wait()
+    order_row[...], slot_ref[...] = slots_of(dest_ref[...], group_count)
+    order_copy = pltpu.make_async_copy(order_row, order_ref, order_sem.at[1])
+    order_copy.start()
     for load in loads:
         load.wait()
+    order_copy.wait()
 
     @pl.loop(0, device_count * group_count)
     def _(slot):
-        pair = order_ref[slot]
+        pair = order_ref[0, slot]
         row, head = pair // head_count, pair % head_count
         staged[slot, 0] = keys_ref[row, head]
         staged[slot, 1] = values_ref[row, head]
@@ -286,31 +312,36 @@
 
 
 def place_kernel(
-    slot_ref, arrived_hbm, attn_ref, mass_ref, keys_out, values_out, attn_out, mass_out,
-    arrived_ref, keys_ref, values_ref, attn_held, in_sem, out_sem,
+    arrived_ref, attn_ref, mass_ref, slot_row, keys_out, values_out, attn_out, mass_out, slot_ref, small_sem, out_sem,
 ):
     row_count, head_count = keys_out.shape[:2]
-    loads = [
-        pltpu.make_async_copy(arrived_hbm.at[:, which], arrived_ref.at[which], in_sem.at[which])
-        for which in range(2)
+    slots = pltpu.make_async_copy(slot_row, slot_ref, small_sem.at[0])
+    slots.start()
+    small = [
+        pltpu.make_async_copy(attn_ref, attn_out, small_sem.at[1]),
+        pltpu.make_async_copy(mass_ref, mass_out, small_sem.at[2]),
     ]
-    for load in loads:
-        load.start()
-    small = pltpu.make_async_copy(attn_ref, attn_held, in_sem.at[2])
-    small.start()
-    mass_out[...] = mass_ref[...]
-    small.wait()
-    out = [pltpu.make_async_copy(attn_held, attn_out, out_sem.at[2, 0])]
-    out[0].start()
-    for which, (held, placed) in enumerate(((keys_ref, keys_out), (values_ref, values_out))):
-        loads[which].wait()
-        for row in range(row_count):
-            for head in range(head_count):
-                held[row, head] = arrived_ref[which, slot_ref[row * head_count + head]]
-            out.append(pltpu.make_async_copy(held.at[row], placed.at[row], out_sem.at[which, row]))
-            out[-1].start()
-    for copy in out:
+    for copy in small:
+        copy.start()
+
+    def copies(row, head, slot):
+        pair = row * head_count + head
+        return [
+            pltpu.make_async_copy(arrived_ref.at[slot, which], placed.at[row, head], out_sem.at[2 * pair + which])
+            for which, placed in enumerate((keys_out, values_out))
+        ]
+
+    slots.wait()
+    for row in range(row_count):
+        for head in range(head_count):
+            for copy in copies(row, head, slot_ref[0, row * head_count + head]):
+                copy.start()
+    for copy in small:
         copy.wait()
+    for row in range(row_count):
+        for head in range(head_count):
+            for copy in copies(row, head, 0):
+                copy.wait()
 
 
 def local(queries, key_cache, value_cache, row_lengths, kept_tiles, tile_dest):
@@ -323,33 +354,33 @@
     pair_rows = STEPS * (QH // head_count)
     owner_rows = group_count * pair_rows
     slots = device_count * group_count
-    assert owner_rows <= LANES and token_span == TILE
-
-    offsets = (tile_dest[:, :, 0] % device_count).reshape(pair_count)
-    index = jnp.arange(pair_count, dtype=jnp.int32)
-    earlier = (index[:, None] > index[None, :]) & (offsets[:, None] == offsets[None, :])
-    slot_of = offsets * group_count + jnp.sum(earlier.astype(jnp.int32), axis=1)
-    hit = slot_of[:, None] == jnp.arange(slots, dtype=jnp.int32)[None, :]
-    order = jnp.sum(jnp.where(hit, index[:, None], 0), axis=0)
-
-    smem = pl.BlockSpec(memory_space=pltpu.SMEM)
+    assert owner_rows <= LANES and token_span == TILE and tile_dest.shape[2] == device_count
+    assert slots <= LANES and pair_count < LANES
+
     vmem = pl.BlockSpec(memory_space=pltpu.VMEM)
     hbm = pl.BlockSpec(memory_space=pltpu.HBM)
     sems = pltpu.SemaphoreType.DMA
-    arrived, attn_out, mass = pl.pallas_call(
+    arrived, attn_out, mass, slot_row = pl.pallas_call(
         functools.partial(main_kernel, device_count, plane, group_count),
         out_shape=(
-            jax.ShapeDtypeStruct((slots, 2, TILE, width), jnp.bfloat16),
-            jax.ShapeDtypeStruct(queries.shape, jnp.bfloat16),
-            jax.ShapeDtypeStruct((row_count, 1, head_count), jnp.float32),
+            pltpu.VMEM((slots, 2, TILE, width), jnp.bfloat16),
+            pltpu.VMEM(queries.shape, jnp.bfloat16),
+            pltpu.VMEM((row_count, 1, head_count), jnp.float32),
+            pltpu.VMEM((1, LANES), jnp.int32),
         ),
-        in_specs=[smem, smem, smem, hbm, hbm, hbm],
-        out_specs=(hbm, vmem, vmem),
+        in_specs=[hbm] * 6,
+        out_specs=(vmem, vmem, vmem, vmem),
         scratch_shapes=[
+            pltpu.SMEM(row_lengths.shape, jnp.int32),
+            pltpu.SMEM((row_count, STEPS, kept_tiles.shape[2]), jnp.int32),
+            pltpu.VMEM(tile_dest.shape, jnp.int32),
+            pltpu.VMEM((1, LANES), jnp.int32),
+            pltpu.SMEM((1, LANES), jnp.int32),
+            sems((2,)),
             pltpu.VMEM(queries.shape, jnp.bfloat16),
             pltpu.VMEM(key_cache.shape, jnp.bfloat16),
             pltpu.VMEM(value_cache.shape, jnp.bfloat16),
-            sems((3,)),
+            sems((5,)),
             pltpu.VMEM((slots, 2, TILE, width), jnp.bfloat16),
             pltpu.VMEM((plane, outer, owner_rows, width), jnp.float32),
             pltpu.VMEM((device_count, LANES, LANES), jnp.float32),
@@ -375,10 +406,13 @@
             sems((2, plane - 1)),
         ],
         compiler_params=pltpu.CompilerParams(
-            collective_id=0, has_side_effects=True, vmem_limit_bytes=63 * 1024 * 1024
+            collective_id=0, has_side_effects=True, vmem_limit_bytes=32 * 1024 * 1024
         ),
         name="attend_and_move",
-    )(order, row_lengths, jnp.swapaxes(kept_tiles, 0, 1), queries, key_cache, value_cache)
+    )(*(
+        pltpu.with_memory_space_constraint(x, pltpu.HBM)
+        for x in (row_lengths, jnp.swapaxes(kept_tiles, 0, 1), tile_dest, queries, key_cache, value_cache)
+    ))
 
     moved_keys, moved_values, attn_out, tile_mass = pl.pallas_call(
         place_kernel,
@@ -388,19 +422,16 @@
             jax.ShapeDtypeStruct(attn_out.shape, attn_out.dtype),
             jax.ShapeDtypeStruct(mass.shape, mass.dtype),
         ),
-        in_specs=[smem, hbm, hbm, vmem],
-        out_specs=(hbm, hbm, hbm, vmem),
+        in_specs=[vmem] * 4,
+        out_specs=(hbm,) * 4,
         scratch_shapes=[
-            pltpu.VMEM((2, slots, TILE, width), jnp.bfloat16),
-            pltpu.VMEM(key_cache.shape, jnp.bfloat16),
-            pltpu.VMEM(value_cache.shape, jnp.bfloat16),
-            pltpu.VMEM(attn_out.shape, attn_out.dtype),
+            pltpu.SMEM((1, LANES), jnp.int32),
             sems((3,)),
-            sems((3, row_count)),
+            sems((2 * pair_count,)),
         ],
-        compiler_params=pltpu.CompilerParams(vmem_limit_bytes=63 * 1024 * 1024),
+        compiler_params=pltpu.CompilerParams(vmem_limit_bytes=8 * 1024 * 1024),
         name="place",
-    )(slot_of, arrived, attn_out, mass)
+    )(arrived, attn_out, mass, slot_row)
     return attn_out, jnp.swapaxes(tile_mass, 1, 2), moved_keys, moved_values
 
 

time: 91 us -> 86.2 us (0.947)
  Pallas kernels: 88.3 us -> 85.5 us
  local copies, waits for them, and re-layouts: 0.99 us -> 0 us
    pallas_call x1, Pallas kernels: 5.18 us -> 3.05 us  [local(): pl.pallas_call(place_kernel, out_shape=(jax.ShapeDtypeStruct(key_cache.sh...]
where the time goes in v2:
time: 86.2 us; the launch traced here: 86.1 us
  Pallas kernels  85.5 us (99%)
    pallas_call x1, Pallas kernels, local(): pl.pallas_call(functools.partial(main_kernel, device_count, plane, group_...  82.4 us
    pallas_call x1, Pallas kernels, local(): pl.pallas_call(place_kernel, out_shape=(jax.ShapeDtypeStruct(key_cache.sh...  3.05 us

profile of v2, /device:TPU:9, one launch (start us, length us, event | category | flops | bytes accessed | tf_op | source)
XLA Modules:
  0.0 86.1 jit_solution(10123529955718429509)
XLA Ops:
  0.6 82.4 %attend_and_move.1 = (bf16[48,2,128,128]{3,2,1,0:T(8,128)(2,1)S(1)}, bf16[4,6,64,128]{3,2,1,0:T(8,128)(2,1)S(1)}, f32[6,1,8]{2,1,0:T(1,128)S(1)}, s32[1,128]{1,0:T(1,128)S(1)}) custom-call(s32[6]{0:T(128)} %lengths_hbm.1, s32[6,4,16]{2,1,0:T(4,128)} %bitcast.2, s32[6,8,16]{2,1,0:T(8,128)} %dest_hbm.1, bf16[4,6,64,128]{3,2,1,0:T(8,128)(2,1)} %queries_hbm.1, ...), custom_call_target="tpu_custom_call" | custom-call | tf_op jit(solution)/shard_map/attend_and_move/pallas_call | solution.py:363
  83.0 3.0 %place.1 = (bf16[6,8,128,128]{3,2,1,0:T(8,128)(2,1)}, bf16[6,8,128,128]{3,2,1,0:T(8,128)(2,1)}, bf16[4,6,64,128]{3,2,1,0:T(8,128)(2,1)}, f32[6,1,8]{2,1,0:T(1,128)}) custom-call(bf16[48,2,128,128]{3,2,1,0:T(8,128)(2,1)S(1)} %get-tuple-element.12.arrived_ref, bf16[4,6,64,128]{3,2,1,0:T(8,128)(2,1)S(1)} %get-tuple-element.13.attn_ref, ...), custom_call_target="tpu_custom_call" | custom-call | tf_op jit(solution)/shard_map/place/pallas_call | solution.py:417
